TPU v7x, 256 devices: a whole 4x4x8 slice. The times are simulated.
256 devices in a mesh: row: 64 (over z_hi, y, x), rep: 4 (over z_lo, core).
Axes of the slice: x: 4, y: 4, z: 8 (z_hi: 4, z_lo: 2; z = z_hi * 2 + z_lo), core: 2. Of those that a mesh axis runs over, the one named last changes fastest.
Arguments:
- features: bfloat16 [32768, 128], P('row'), may hold values from -6 to 6
- weight_one: bfloat16 [128, 128], replicated, may hold values from -0.5 to 0.5
- weight_two: bfloat16 [128, 128], replicated, may hold values from -0.5 to 0.5
- cotangent: bfloat16 [32768, 128], P('row'), may hold values from -0.03125 to 0.03125
- adj_tiles: bfloat16 [64, 64, 16, 128, 128], P('row', 'rep'), may hold values from -0.09375 to 0.09375
- tile_rows: int32 [64, 64, 16], P('row', 'rep'), may hold values from 0 to 3, as said below
- tile_cols: int32 [64, 64, 16], P('row', 'rep'), may hold values from 0 to 3
- tile_counts: int32 [64, 64], P('row', 'rep'), may hold values from 0 to 16, as said below
Outputs:
- output: bfloat16 [32768, 128], P('row')
- grad_one: float32 [128, 128], replicated
- grad_two: float32 [128, 128], replicated
Inputs may be any that keep to these rules, and one draw needn't show every extreme that they name: Only slots 0 to tile_counts[b, s] - 1 of block-row b and section s are live; the other slots carry arbitrary tiles and indices that are not part of A. Section b of block-row b holds 16 live slots; many other sections hold none. `tile_rows`: the (row, column) pairs of the slots of one block-row and section are distinct.
All inputs are finite; a program needn't handle non-finite values.
Results may differ from a plain program's by a relative error of at most 0.0065.
Values may be sent and summed in bfloat16 or wider, within the bound.
A program may use at most 192 MiB of HBM per device.

v0:
```python
from functools import partial
import jax
import jax.numpy as jnp
from jax import lax
from jax.sharding import PartitionSpec as P

TILE = 128


def gelu_value(values):
    return values * 0.5 * (1.0 + lax.erf(values * 0.7071067811865476))


def gelu_slope(values):
    normal_cdf = 0.5 * (1.0 + lax.erf(values * 0.7071067811865476))
    return normal_cdf + values * jnp.exp(-0.5 * values * values) * 0.3989422804014327


def row_contract(left, right):
    return lax.dot_general(
        left, right, (((0,), (0,)), ((), ())), preferred_element_type=jnp.float32
    )


def section_work(running, pieces, section_tiles, section_rows, section_cols, live_count):
    slot_total = section_tiles.shape[0]
    count_tiles = running.shape[0]
    sources = jnp.take(pieces, section_cols, axis=0)
    products = jnp.einsum(
        "mij,mjf->mif", section_tiles, sources, preferred_element_type=jnp.float32
    )
    live_mask = jnp.arange(slot_total, dtype=jnp.int32) < live_count
    onehot = jnp.where(
        live_mask[:, None]
        & (section_rows[:, None] == jnp.arange(count_tiles, dtype=jnp.int32)[None, :]),
        1.0,
        0.0,
    ).astype(jnp.float32)
    return running + jnp.einsum("mk,mif->kif", onehot, products, precision=lax.Precision.HIGHEST)


def propagate(tile_data, row_ids, col_ids, live_counts, own_block):
    section_total = tile_data.shape[0]
    block_rows = own_block.shape[0]
    count_tiles = block_rows // TILE
    width = own_block.shape[1]
    first_section = lax.axis_index("rep") * section_total

    def pick(section_id):
        return (
            lax.dynamic_index_in_dim(tile_data, section_id, 0, keepdims=False),
            lax.dynamic_index_in_dim(row_ids, section_id, 0, keepdims=False),
            lax.dynamic_index_in_dim(col_ids, section_id, 0, keepdims=False),
            lax.dynamic_index_in_dim(live_counts, section_id, 0, keepdims=False),
        )

    zeros = jnp.zeros((count_tiles, TILE, width), jnp.float32)
    kept_total = section_total * block_rows
    kept_base = first_section * block_rows
    empty = jnp.zeros((kept_total, width), own_block.dtype)
    piece = lax.all_gather(own_block, "row", axis=0, tiled=True)
    piece_rows = piece.shape[0]
    padding = jnp.zeros((piece_rows, width), empty.dtype)
    widened = jnp.concatenate([padding, empty, padding], axis=0)
    offset = jnp.clip(jnp.int32(0) - kept_base + piece_rows, 0, kept_total + piece_rows)
    widened = lax.dynamic_update_slice_in_dim(widened, piece, offset, 0)
    kept = widened[piece_rows : piece_rows + kept_total]
    kept = kept.reshape(section_total, count_tiles, TILE, width)

    def kept_step(section_id, running):
        pieces = lax.dynamic_index_in_dim(kept, section_id, 0, keepdims=False)
        return section_work(running, pieces, *pick(section_id))

    summed = lax.fori_loop(0, section_total, kept_step, zeros)
    return summed.reshape(block_rows, width)


def whole_sum(partial_rows):
    return lax.psum(partial_rows, "rep")


def per_device(
    features, weight_one, weight_two, cotangent, adj_tiles, tile_rows, tile_cols, tile_counts
):
    spread = partial(propagate, adj_tiles[0], tile_rows[0], tile_cols[0], tile_counts[0])
    d_two = lax.dot_general(
        cotangent, weight_two, (((1,), (1,)), ((), ())), preferred_element_type=jnp.float32
    ).astype(jnp.bfloat16)
    s_one = whole_sum(spread(features)).astype(jnp.bfloat16)
    pre_one = jnp.dot(s_one, weight_one, preferred_element_type=jnp.float32)
    hidden = gelu_value(pre_one).astype(jnp.bfloat16)
    s_two = whole_sum(spread(hidden)).astype(jnp.bfloat16)
    output = jnp.dot(s_two, weight_two, preferred_element_type=jnp.float32).astype(jnp.bfloat16)
    grad_two = lax.psum(row_contract(s_two, cotangent), "row")
    d_hidden = whole_sum(spread(d_two))
    d_pre = (d_hidden * gelu_slope(pre_one)).astype(jnp.bfloat16)
    grad_one = lax.psum(row_contract(s_one, d_pre), "row")
    return (output, grad_one, grad_two)


def solution(mesh):
    placed = (
        P("row", None),
        P(),
        P(),
        P("row", None),
        P("row", "rep", None, None, None),
        P("row", "rep", None),
        P("row", "rep", None),
        P("row", "rep"),
    )
    return jax.shard_map(
        per_device,
        mesh=mesh,
        in_specs=placed,
        out_specs=(P("row", None), P(), P()),
        check_vma=False,
    )
```

profile of v0, /device:TPU:2, one launch (start us, length us, event | category | flops | bytes accessed | tf_op | source)
XLA Modules:
  0.0 1363.7 jit_solution(14181095154365439595)
XLA Ops:
  8.1 1.6 convolution_convert_fusion
  10.6 3.9 broadcast.50
  14.4 15.8 %pad_maximum_fusion = bf16[73728,128]{1,0:T(8,128)(2,1)S(1)} fusion(bf16[32768,128]{1,0:T(8,128)(2,1)} %broadcast.50, bf16[73728]{0:T(1024)(128)(2,1)S(1)} %pad.1.clone), kind=kLoop, calls=%fused_computation.90 | loop fusion | flops 56623104 | bytes 27410432 | tf_op jit(solution)/shard_map/concatenate | solution.py:64
  30.2 6.4 copy.46
  36.6 5.8 copy-done.1
  42.4 6.5 copy.38
  48.8 73.8 %all-gather.8.cloned.1.call-done = bf16[32768,128]{1,0:T(8,128)(2,1)} async-done(((bf16[512,128]{1,0:T(8,128)(2,1)}), bf16[32768,128]{1,0:T(8,128)(2,1)}) %all-gather.8.cloned.1.call-update) | async-done | bytes 8388624 | tf_op jit(solution)/shard_map/all_gather | solution.py:61
  122.6 39.0 %dynamic_update_slice.11 = bf16[73728,128]{1,0:T(8,128)(2,1)} dynamic-update-slice(bf16[73728,128]{1,0:T(8,128)(2,1)} %copy.46, bf16[32768,128]{1,0:T(8,128)(2,1)} %all-gather.8.cloned.1.call-done, s32[]{:T(128)S(6)} %min.6, s32[]{:T(128)} %constant.163.clone.1) | dynamic-update-slice | bytes 16777220 | tf_op jit(solution)/shard_map/dynamic_update_slice | solution.py:66
  161.7 3.0 slice.20
  164.7 113.0 %while.44 = (s32[]{:T(128)}, f32[4,128,128]{2,0,1:T(4,128)S(1)}, s32[16]{0:T(128)S(1)}, s32[16,16]{1,0:T(8,128)}, bf16[16,16,128,128]{3,2,1,0:T(8,128)(2,1)}, /*...) while((s32[]{:T(128)}, f32[4,128,128]{2,0,1:T(4,128)S(1)}, ...), condition=%wide.region_7.9_spmd.clone, body=%wide.region_6.8_spmd.clone.sunk | while | flops 80086320 | bytes 4985487 | solution.py:74
  176.0 1.5 fusion.124
  183.1 1.4 fusion.124
  197.2 1.4 fusion.124
  204.3 1.4 fusion.124
  218.4 1.4 fusion.124
  232.5 1.4 fusion.124
  278.5 39.1 %dynamic_update_slice.9 = bf16[73728,128]{1,0:T(8,128)(2,1)} dynamic-update-slice(bf16[73728,128]{1,0:T(8,128)(2,1)} %copy-done.1, bf16[32768,128]{1,0:T(8,128)(2,1)} %all-gather.4.cloned.1.call-done, s32[]{:T(128)S(6)} %min.6, s32[]{:T(128)} %constant.163.clone.1) | dynamic-update-slice | bytes 16777220 | tf_op jit(solution)/shard_map/dynamic_update_slice | solution.py:66
  317.6 1.7 slice.18
  319.3 98.5 %while.42 = (s32[]{:T(128)}, f32[4,128,128]{2,0,1:T(4,128)S(1)}, s32[16]{0:T(128)S(1)}, s32[16,16]{1,0:T(8,128)}, bf16[16,16,128,128]{3,2,1,0:T(8,128)(2,1)}, /*...) while((s32[]{:T(128)}, f32[4,128,128]{2,0,1:T(4,128)S(1)}, ...), condition=%wide.region_1.3_spmd.clone, body=%wide.region_0.2_spmd.clone.sunk | while | flops 80086320 | bytes 4985487 | solution.py:74
  335.0 1.4 fusion.112
  341.1 1.4 fusion.112
  347.3 1.4 fusion.112
  353.4 1.4 fusion.112
  359.6 1.4 fusion.112
  365.8 1.4 fusion.112
  371.9 1.4 fusion.112
  378.1 1.4 fusion.112
  384.2 1.4 fusion.112
  396.5 1.4 fusion.112
  408.9 1.4 fusion.112
  417.9 21.4 %all-reduce.9 = bf16[512,128]{1,0:T(8,128)(2,1)S(1)} all-reduce(f32[512,128]{1,0:T(8,128)S(1)} %bitcast.102), channel_id=1, replica_groups=mesh['row'=64,'rep'=4] {'rep'}, use_global_device_ids=true, to_apply=%region_2.4 | all-reduce | flops 65536 | bytes 393216 | tf_op jit(solution)/shard_map/psum | solution.py:79
  440.3 1.9 fusion.69
  442.1 104.2 %all-gather.6.cloned.1.call-done = bf16[32768,128]{1,0:T(8,128)(2,1)} async-done(((bf16[512,128]{1,0:T(8,128)(2,1)}), bf16[32768,128]{1,0:T(8,128)(2,1)}) %all-gather.6.cloned.1.call-update) | async-done | bytes 8388624 | tf_op jit(solution)/shard_map/all_gather | solution.py:61
  546.3 39.1 %dynamic_update_slice.10 = bf16[73728,128]{1,0:T(8,128)(2,1)} dynamic-update-slice(bf16[73728,128]{1,0:T(8,128)(2,1)} %copy.38, bf16[32768,128]{1,0:T(8,128)(2,1)} %all-gather.6.cloned.1.call-done, s32[]{:T(128)S(6)} %min.6, s32[]{:T(128)} %constant.163.clone.1) | dynamic-update-slice | bytes 16777220 | tf_op jit(solution)/shard_map/dynamic_update_slice | solution.py:66
  585.4 1.7 slice.19
  587.2 98.5 %while.43 = (s32[]{:T(128)}, f32[4,128,128]{2,0,1:T(4,128)S(1)}, s32[16]{0:T(128)S(1)}, s32[16,16]{1,0:T(8,128)}, bf16[16,16,128,128]{3,2,1,0:T(8,128)(2,1)}, /*...) while((s32[]{:T(128)}, f32[4,128,128]{2,0,1:T(4,128)S(1)}, ...), condition=%wide.region_4.6_spmd.clone, body=%wide.region_3.5_spmd.clone.sunk | while | flops 80086320 | bytes 4985487 | solution.py:74
  609.0 1.4 fusion.118
  621.3 1.4 fusion.118
  627.5 1.4 fusion.118
  645.9 1.4 fusion.118
  652.1 1.4 fusion.118
  658.2 1.4 fusion.118
  664.4 1.4 fusion.118
  670.5 1.4 fusion.118
  685.7 21.3 %all-reduce.10 = bf16[512,128]{1,0:T(8,128)(2,1)S(1)} all-reduce(f32[512,128]{1,0:T(8,128)S(1)} %bitcast.103), channel_id=1, replica_groups=mesh['row'=64,'rep'=4] {'rep'}, use_global_device_ids=true, to_apply=%region_5.7 | all-reduce | flops 65536 | bytes 393216 | tf_op jit(solution)/shard_map/psum | solution.py:79
  708.8 645.5 %all-reduce.8.cloned.1.call-done = (f32[128,128]{1,0:T(8,128)}, f32[128,128]{1,0:T(8,128)}) async-done(((f32[128,128]{1,0:T(8,128)}, f32[128,128]{1,0:T(8,128)}), (f32[128,128]{1,0:T(8,128)}, f32[128,128]{1,0:T(8,128)})) %all-reduce.8.cloned.1.call-update) | async-done | bytes 131088 | tf_op jit(solution)/shard_map/psum | solution.py:97
  1354.2 1.5 copy.58
  1355.7 1.5 copy.59
  (441 shorter events, 277.4 us)
Async XLA Ops:
  7.2 0.9 copy-start
  7.2 115.4 %all-gather.8.cloned.1.call-start = ((), (), s32[]{:S(2)}) async-start(), calls=%async_computation.2 | async-start | bytes 8519680 | tf_op jit(solution)/shard_map/all_gather | solution.py:61
  9.7 268.8 %all-gather.4.cloned.1.call-start = ((), (), s32[]{:S(2)}) async-start(), calls=%async_computation | async-start | bytes 8519680 | tf_op jit(solution)/shard_map/all_gather | solution.py:61
  10.5 429.8 %all-reduce.6.cloned.1.call-start = ((), (), s32[]{:S(2)}) async-start(), calls=%async_computation.3 | async-start | bytes 524288 | tf_op jit(solution)/shard_map/psum | solution.py:79
  30.2 12.2 copy-start.1
  48.8 115.9 %copy-start.2 = (f32[4,128,128]{2,0,1:T(4,128)S(1)}, f32[4,128,128]{2,0,1:T(4,128)}, u32[]{:S(2)}) copy-start(f32[4,128,128]{2,0,1:T(4,128)} %custom-call.2) | copy-start | bytes 786436
  48.8 115.9 %copy-start.5 = (s32[1,16]{1,0:T(1,128)S(1)}, s32[1,16]{1,0:T(1,128)}, u32[]{:S(2)}) copy-start(s32[1,16]{1,0:T(1,128)} %param.23) | copy-start | bytes 196
  278.4 267.9 %all-gather.6.cloned.1.call-start = ((), (), s32[]{:S(2)}) async-start(), calls=%async_computation.1 | async-start | bytes 8519680 | tf_op jit(solution)/shard_map/all_gather | solution.py:61
  319.3 120.0 %copy-start.4 = (bf16[128,128]{1,0:T(8,128)(2,1)S(1)}, bf16[128,128]{1,0:T(8,128)(2,1)}, u32[]{:S(2)}) copy-start(bf16[128,128]{1,0:T(8,128)(2,1)} %param.17) | copy-start | bytes 98308
  440.2 914.0 %all-reduce.8.cloned.1.call-start = ((), (), s32[]{:S(2)}) async-start(), calls=%async_computation.4 | async-start | bytes 262144 | tf_op jit(solution)/shard_map/psum | solution.py:97
  587.2 120.8 %copy-start.3 = (bf16[128,128]{1,0:T(8,128)(2,1)S(1)}, bf16[128,128]{1,0:T(8,128)(2,1)}, u32[]{:S(2)}) copy-start(bf16[128,128]{1,0:T(8,128)(2,1)} %param.18) | copy-start | bytes 98308
Sparse Core Ops, SparseCore 0:
  11.9 110.6 all-gather.7
  125.9 113.1 all-gather.3
  278.5 46.1 all-reduce.5
  440.3 105.9 all-gather.5
  708.0 646.1 all-reduce.7
where the time goes:
time: 1370 us; the launch traced here: 1360 us
  waiting for transfers between devices  824 us (60%)
  local copies, waits for them, and re-layouts  259 us (19%)
  matrix products  141 us (10%)
  other arithmetic  80.6 us (6%)
  blocking collectives  42.8 us (3%)
  between operations  14 us (1%)
    psum x1, waiting for transfers between devices, per_device(): grad_one = lax.psum(row_contract(s_one, d_pre), 'row')  645 us
    all_gather x3, waiting for transfers between devices, propagate(): piece = lax.all_gather(own_block, 'row', axis=0, tiled=True)  178 us
    dynamic_update_slice x3, local copies, waits for them, and re-layouts, propagate(): widened = lax.dynamic_update_slice_in_dim(widened, piece, offset, 0)  117 us
    dot_general x48, matrix products, section_work(): jnp.einsum('mij,mjf->mif', section_tiles, sources, preferred_element_type...  68 us
    dot_general x48, matrix products, section_work(): jnp.einsum('mk,mif->kif', onehot, products, precision=lax.Precision.HIGHEST)  66.7 us
    psum x2, blocking collectives, whole_sum(): return lax.psum(partial_rows, 'rep')  42.8 us
    eq x48, local copies, waits for them, and re-layouts, section_work(): section_rows[:, None] == jnp.arange(count_tiles, dtype=jnp.int32)[None, :]  33.5 us
    and x48, other arithmetic, section_work(): sources = jnp.take(pieces, section_cols, axis=0)  33.4 us
  transfers between devices with their start and end apart: 5, of which 3 were waited for; matrix products, arithmetic and copies ran while one was open for 24% of the time, Pallas kernels for 0%

commit v1 on v0

--- a/solution.py
+++ b/solution.py
@@ -1,3 +1,4 @@
+import functools
 from functools import partial
 import jax
 import jax.numpy as jnp
@@ -5,6 +6,14 @@
 from jax.sharding import PartitionSpec as P
 
 TILE = 128
+
+
+def place_the_rounds(row_data, link_axis):
+    carry = jnp.stack([row_data for _ in range(lax.axis_size(link_axis))], axis=0)
+    return jnp.concatenate(lax.all_to_all(carry, link_axis, 0, 0), 0)
+
+
+lead_layers_all_for = functools.partial(place_the_rounds, link_axis="row")
 
 
 def gelu_value(values):
@@ -58,7 +67,7 @@
     kept_total = section_total * block_rows
     kept_base = first_section * block_rows
     empty = jnp.zeros((kept_total, width), own_block.dtype)
-    piece = lax.all_gather(own_block, "row", axis=0, tiled=True)
+    piece = lead_layers_all_for(own_block)
     piece_rows = piece.shape[0]
     padding = jnp.zeros((piece_rows, width), empty.dtype)
     widened = jnp.concatenate([padding, empty, padding], axis=0)

time: 1370 us -> 1620 us (1.18)
  waiting for transfers between devices: 824 us -> 1020 us
  starting transfers between devices: 0.2 us -> 42.3 us
  local copies, waits for them, and re-layouts: 259 us -> 290 us
    all_to_all x0 -> x3, waiting for transfers between devices: none -> 296 us  [place_the_rounds(): return jnp.concatenate(lax.all_to_all(carry, link_axis, 0, 0), 0)]
    all_gather x3 -> x0, waiting for transfers between devices: 178 us -> none  [propagate(): piece = lax.all_gather(own_block, 'row', axis=0, tiled=True)]
    psum x1, waiting for transfers between devices: 0.02 us -> 68 us  [whole_sum(): return lax.psum(partial_rows, 'rep')]
    all_to_all x0 -> x3, starting transfers between devices: none -> 42 us  [place_the_rounds(): return jnp.concatenate(lax.all_to_all(carry, link_axis, 0, 0), 0)]
  transfers between devices with their start and end apart: 5 -> 5, of which waited for: 3 -> 5; matrix products, arithmetic and copies ran while one was open for 24% -> 12% of each run, Pallas kernels for 0% -> 0%
where the time goes in v1:
time: 1620 us; the launch traced here: 1610 us
  waiting for transfers between devices  1020 us (63%)
  local copies, waits for them, and re-layouts  290 us (18%)
  matrix products  139 us (9%)
  other arithmetic  80.6 us (5%)
  starting transfers between devices  42.3 us (3%)
  blocking collectives  27.1 us (2%)
    psum x1, waiting for transfers between devices, per_device(): grad_one = lax.psum(row_contract(s_one, d_pre), 'row')  652 us
    all_to_all x3, waiting for transfers between devices, place_the_rounds(): return jnp.concatenate(lax.all_to_all(carry, link_axis, 0, 0), 0)  296 us
    dynamic_update_slice x3, local copies, waits for them, and re-layouts, propagate(): widened = lax.dynamic_update_slice_in_dim(widened, piece, offset, 0)  117 us
    psum x1, waiting for transfers between devices, whole_sum(): return lax.psum(partial_rows, 'rep')  68 us
    dot_general x48, matrix products, section_work(): jnp.einsum('mij,mjf->mif', section_tiles, sources, preferred_element_type...  67.9 us
    dot_general x48, matrix products, section_work(): jnp.einsum('mk,mif->kif', onehot, products, precision=lax.Precision.HIGHEST)  66.7 us
    all_to_all x3, starting transfers between devices, place_the_rounds(): return jnp.concatenate(lax.all_to_all(carry, link_axis, 0, 0), 0)  42 us
    eq x48, local copies, waits for them, and re-layouts, section_work(): section_rows[:, None] == jnp.arange(count_tiles, dtype=jnp.int32)[None, :]  33.5 us
  transfers between devices with their start and end apart: 5, of which 5 were waited for; matrix products, arithmetic and copies ran while one was open for 12% of the time, Pallas kernels for 0%

profile of v1, /device:TPU:2, one launch (start us, length us, event | category | flops | bytes accessed | tf_op | source)
XLA Modules:
  0.0 1611.4 jit_solution(6650138017145126597)
XLA Ops:
  9.0 5.3 stack.8
  14.3 15.0 all-to-all-start.2
  29.3 186.3 %all-to-all-done.2 = bf16[64,512,128]{2,1,0:T(8,128)(2,1)} async-done(((bf16[64,512,128]{2,1,0:T(8,128)(2,1)}), bf16[64,512,128]{2,1,0:T(8,128)(2,1)}, u32[]{:S(2)}, u32[]{:S(2)}) %all-to-all-start.2) | async-done | bytes 8388640 | tf_op jit(solution)/shard_map/all_to_all | solution.py:13
  215.6 5.3 stack.6
  220.9 7.5 all-to-all-start
  228.4 3.9 broadcast.56
  232.3 15.8 pad_maximum_fusion
  248.1 6.4 copy.46
  254.4 5.7 copy-done.1
  260.2 6.5 copy.38
  266.6 39.0 %dynamic_update_slice.11 = bf16[73728,128]{1,0:T(8,128)(2,1)} dynamic-update-slice(bf16[73728,128]{1,0:T(8,128)(2,1)} %copy.46, bf16[32768,128]{1,0:T(8,128)(2,1)} %bitcast.10, s32[]{:T(128)S(6)} %min.6, s32[]{:T(128)} %constant.163.clone.1) | dynamic-update-slice | bytes 16777220 | tf_op jit(solution)/shard_map/dynamic_update_slice | solution.py:75
  305.7 3.1 slice.20
  308.7 103.9 %all-to-all-done = bf16[64,512,128]{2,1,0:T(8,128)(2,1)} async-done(((bf16[64,512,128]{2,1,0:T(8,128)(2,1)}), bf16[64,512,128]{2,1,0:T(8,128)(2,1)}, u32[]{:S(2)}, u32[]{:S(2)}) %all-to-all-start) | async-done | bytes 8388640 | tf_op jit(solution)/shard_map/all_to_all | solution.py:13
  412.6 39.1 %dynamic_update_slice.9 = bf16[73728,128]{1,0:T(8,128)(2,1)} dynamic-update-slice(bf16[73728,128]{1,0:T(8,128)(2,1)} %copy-done.1, bf16[32768,128]{1,0:T(8,128)(2,1)} %bitcast.3, s32[]{:T(128)S(6)} %min.6, s32[]{:T(128)} %constant.163.clone.1) | dynamic-update-slice | bytes 16777220 | tf_op jit(solution)/shard_map/dynamic_update_slice | solution.py:75
  451.7 3.0 slice.18
  454.8 112.8 %while.42 = (s32[]{:T(128)}, f32[4,128,128]{2,0,1:T(4,128)S(1)}, s32[16]{0:T(128)S(1)}, s32[16,16]{1,0:T(8,128)}, bf16[16,16,128,128]{3,2,1,0:T(8,128)(2,1)}, /*...) while((s32[]{:T(128)}, f32[4,128,128]{2,0,1:T(4,128)S(1)}, ...), condition=%wide.region_1.3_spmd.clone, body=%wide.region_0.2_spmd.clone.sunk | while | flops 80086320 | bytes 4985487 | solution.py:83
  459.0 1.4 fusion.112
  473.1 1.4 fusion.112
  536.6 1.4 fusion.112
  557.7 1.4 fusion.112
  567.6 13.6 all-reduce.9
  581.5 5.3 stack.7
  586.8 19.5 %all-to-all-start.1 = ((bf16[64,512,128]{2,1,0:T(8,128)(2,1)}), bf16[64,512,128]{2,1,0:T(8,128)(2,1)}, u32[]{:S(2)}, u32[]{:S(2)}) async-start(bf16[64,512,128]{2,1,0:T(8,128)(2,1)} %stack.7), calls=%async_computation.1 | async-start | bytes 16777216 | tf_op jit(solution)/shard_map/all_to_all | solution.py:13
  606.5 112.8 %while.44 = (s32[]{:T(128)}, f32[4,128,128]{2,0,1:T(4,128)S(1)}, s32[16]{0:T(128)S(1)}, s32[16,16]{1,0:T(8,128)}, bf16[16,16,128,128]{3,2,1,0:T(8,128)(2,1)}, /*...) while((s32[]{:T(128)}, f32[4,128,128]{2,0,1:T(4,128)S(1)}, ...), condition=%wide.region_7.9_spmd.clone, body=%wide.region_6.8_spmd.clone.sunk | while | flops 80086320 | bytes 4985487 | solution.py:83
  617.8 1.4 fusion.124
  646.0 1.4 fusion.124
  720.2 68.0 %all-reduce.6.cloned.1.call-done = f32[512,128]{1,0:T(8,128)} async-done(((f32[512,128]{1,0:T(8,128)}), f32[512,128]{1,0:T(8,128)}) %all-reduce.6.cloned.1.call-update) | async-done | bytes 262160 | tf_op jit(solution)/shard_map/psum | solution.py:88
  788.2 1.9 fusion.69
  790.1 5.5 all-to-all-done.1
  795.6 39.1 %dynamic_update_slice.10 = bf16[73728,128]{1,0:T(8,128)(2,1)} dynamic-update-slice(bf16[73728,128]{1,0:T(8,128)(2,1)} %copy.38, bf16[32768,128]{1,0:T(8,128)(2,1)} %bitcast.7, s32[]{:T(128)S(6)} %min.6, s32[]{:T(128)} %constant.163.clone.1) | dynamic-update-slice | bytes 16777220 | tf_op jit(solution)/shard_map/dynamic_update_slice | solution.py:75
  834.7 1.7 slice.19
  836.4 98.5 %while.43 = (s32[]{:T(128)}, f32[4,128,128]{2,0,1:T(4,128)S(1)}, s32[16]{0:T(128)S(1)}, s32[16,16]{1,0:T(8,128)}, bf16[16,16,128,128]{3,2,1,0:T(8,128)(2,1)}, /*...) while((s32[]{:T(128)}, f32[4,128,128]{2,0,1:T(4,128)S(1)}, ...), condition=%wide.region_4.6_spmd.clone, body=%wide.region_3.5_spmd.clone.sunk | while | flops 80086320 | bytes 4985487 | solution.py:83
  839.7 1.4 fusion.118
  845.9 1.4 fusion.118
  852.1 1.4 fusion.118
  870.5 1.4 fusion.118
  876.7 1.4 fusion.118
  882.8 1.4 fusion.118
  889.0 1.4 fusion.118
  895.1 1.4 fusion.118
  913.6 1.4 fusion.118
  919.8 1.4 fusion.118
  925.9 1.4 fusion.118
  932.1 1.4 fusion.118
  934.9 13.5 all-reduce.10
  950.1 651.5 %all-reduce.8.cloned.1.call-done = (f32[128,128]{1,0:T(8,128)}, f32[128,128]{1,0:T(8,128)}) async-done(((f32[128,128]{1,0:T(8,128)}, f32[128,128]{1,0:T(8,128)}), (f32[128,128]{1,0:T(8,128)}, f32[128,128]{1,0:T(8,128)})) %all-reduce.8.cloned.1.call-update) | async-done | bytes 131088 | tf_op jit(solution)/shard_map/psum | solution.py:106
  1601.7 1.5 copy.58
  1603.1 1.5 copy.59
  (443 shorter events, 301.3 us)
Async XLA Ops:
  7.2 0.9 copy-start
  14.3 201.3 %copy-start.3 = (bf16[512,128]{1,0:T(8,128)(2,1)S(1)}, bf16[512,128]{1,0:T(8,128)(2,1)}, u32[]{:S(2)}) copy-start(bf16[512,128]{1,0:T(8,128)(2,1)} %param.16) | copy-start | bytes 393220
  14.3 201.3 %all-to-all-start.2 = ((bf16[64,512,128]{2,1,0:T(8,128)(2,1)}), bf16[64,512,128]{2,1,0:T(8,128)(2,1)}, u32[]{:S(2)}, u32[]{:S(2)}) async-start(bf16[64,512,128]{2,1,0:T(8,128)(2,1)} %stack.8), calls=%async_computation.2 | async-start | bytes 16777216 | tf_op jit(solution)/shard_map/all_to_all | solution.py:13
  220.9 191.7 %all-to-all-start = ((bf16[64,512,128]{2,1,0:T(8,128)(2,1)}), bf16[64,512,128]{2,1,0:T(8,128)(2,1)}, u32[]{:S(2)}, u32[]{:S(2)}) async-start(bf16[64,512,128]{2,1,0:T(8,128)(2,1)} %stack.6), calls=%async_computation | async-start | bytes 16777216 | tf_op jit(solution)/shard_map/all_to_all | solution.py:13
  248.1 12.1 copy-start.1
  412.6 42.1 %copy-start.2 = (f32[4,128,128]{2,0,1:T(4,128)S(1)}, f32[4,128,128]{2,0,1:T(4,128)}, u32[]{:S(2)}) copy-start(f32[4,128,128]{2,0,1:T(4,128)} %custom-call) | copy-start | bytes 786436
  412.6 42.1 %copy-start.6 = (s32[1,16]{1,0:T(1,128)S(1)}, s32[1,16]{1,0:T(1,128)}, u32[]{:S(2)}) copy-start(s32[1,16]{1,0:T(1,128)} %param.23) | copy-start | bytes 196
  454.8 126.5 %copy-start.5 = (bf16[128,128]{1,0:T(8,128)(2,1)S(1)}, bf16[128,128]{1,0:T(8,128)(2,1)}, u32[]{:S(2)}) copy-start(bf16[128,128]{1,0:T(8,128)(2,1)} %param.17) | copy-start | bytes 98308
  586.8 208.8 %all-to-all-start.1 = ((bf16[64,512,128]{2,1,0:T(8,128)(2,1)}), bf16[64,512,128]{2,1,0:T(8,128)(2,1)}, u32[]{:S(2)}, u32[]{:S(2)}) async-start(bf16[64,512,128]{2,1,0:T(8,128)(2,1)} %stack.7), calls=%async_computation.1 | async-start | bytes 16777216 | tf_op jit(solution)/shard_map/all_to_all | solution.py:13
  606.3 181.9 %all-reduce.6.cloned.1.call-start = ((), (), s32[]{:S(2)}) async-start(), calls=%async_computation.3 | async-start | bytes 524288 | tf_op jit(solution)/shard_map/psum | solution.py:88
  720.1 881.5 %all-reduce.8.cloned.1.call-start = ((), (), s32[]{:S(2)}) async-start(), calls=%async_computation.4 | async-start | bytes 262144 | tf_op jit(solution)/shard_map/psum | solution.py:106
  836.4 112.9 %copy-start.4 = (bf16[128,128]{1,0:T(8,128)(2,1)S(1)}, bf16[128,128]{1,0:T(8,128)(2,1)}, u32[]{:S(2)}) copy-start(bf16[128,128]{1,0:T(8,128)(2,1)} %param.18) | copy-start | bytes 98308
Sparse Core Ops, SparseCore 0:
  720.2 67.9 all-reduce.5
  949.4 652.1 all-reduce.7
